TPU v7x, 256 devices: a whole 4x4x8 slice. The times are simulated.
256 devices in a mesh: space: 64 (over z, y, core), tm: 4 (over x).
Axes of the slice: x: 4, y: 4, z: 8, core: 2. Of those that a mesh axis runs over, the one named last changes fastest.
Arguments:
- snapshots: bfloat16 [256, 524288], P('tm', 'space'), may hold values from -75 to 75
- prior_basis: bfloat16 [256, 524288], P('tm', 'space'), may hold values from -75 to 75
- mass_factor: bfloat16 [7, 64, 524288], P(None, None, 'space'), may hold values from -1 to 3.2, as said below
- neighbours: int32 [8192, 7], P('space'), may hold values from 0 to 8191, as said below
Outputs:
- merged_basis: bfloat16 [64, 524288], P(None, ('space', 'tm'))
- merged_weighted: bfloat16 [64, 524288], P(None, ('space', 'tm'))
Inputs may be any that keep to these rules, and one draw needn't show every extreme that they name: `mass_factor`: factor entries; the diagonal of each block's own coupling lies in 1.5 to 3. neighbours[i, 0] = i; every entry lies within 8 blocks of i; in every draw some entries lie exactly 8 blocks below and above their block.
All inputs are finite; a program needn't handle non-finite values.
Results may differ from a plain program's by a relative error of at most 0.018.
Values may be sent and summed in bfloat16 or wider, within the bound.
A program may use at most 128 MiB of HBM per device.

v0:
```python
import jax
import jax.numpy as jnp
from jax import lax
from jax.sharding import PartitionSpec as P

BLOCK_DOFS = 64
RANK = 64
NEIGHBOURS = 7
REACH = 8
SUBSPACE_STEPS = 3
LOCAL_BLOCKS = 128


def padded(block, sides, width):
    for axis, dim in sides:
        count = lax.axis_size(axis)
        forward = [(i, i + 1) for i in range(count - 1)]
        backward = [(target, source) for source, target in forward]
        low = lax.ppermute(
            lax.slice_in_dim(block, block.shape[dim] - width, None, axis=dim), axis, forward
        )
        high = lax.ppermute(lax.slice_in_dim(block, 0, width, axis=dim), axis, backward)
        block = jnp.concatenate([low, block, high], axis=dim)
    return block


def partner(block, axis, bit):
    count = lax.axis_size(axis)
    route = []
    for low in range(count):
        high = low | 1 << bit
        if high != low and high < count:
            route += [(low, high), (high, low)]
    return lax.ppermute(block, axis, route)


def weigh_rows(stacked, mass_factor, local_index):
    columns = stacked.shape[0]
    widened = padded(stacked, (("space", 1),), REACH * BLOCK_DOFS)
    blocks = widened.reshape(columns, -1, BLOCK_DOFS)
    picked = jnp.take(blocks, local_index, axis=1)
    factor = mass_factor.reshape(NEIGHBOURS, BLOCK_DOFS, -1, BLOCK_DOFS)
    result = jnp.einsum("cbkq,kqbr->cbr", picked, factor, preferred_element_type=jnp.float32)
    return result.reshape(columns, -1).astype(jnp.bfloat16)


def compress(gram_total):
    highest = lax.Precision.HIGHEST
    order_size = gram_total.shape[0]
    weights = jnp.eye(order_size, RANK, dtype=jnp.float32)
    for repeat in range(SUBSPACE_STEPS):
        product = jnp.dot(gram_total, weights, precision=highest)
        inner_gram = jnp.dot(
            product.T, jnp.dot(gram_total, product, precision=highest), precision=highest
        )
        scales = jnp.sqrt(jnp.diagonal(inner_gram))
        factor_lower = jnp.linalg.cholesky(inner_gram / (scales[:, None] * scales[None, :]))
        normed = product / scales[None, :]
        weights = lax.linalg.triangular_solve(
            factor_lower, normed, left_side=False, lower=True, transpose_a=True
        )
    product = jnp.dot(gram_total, weights, precision=highest)
    lengths = jnp.sqrt(jnp.sum(product * product, axis=0) + 1e-06)
    return (weights * lengths[None, :]).astype(jnp.bfloat16)


def coefficients_of(weighted):
    local_gram = jnp.dot(weighted, weighted.T, preferred_element_type=jnp.float32)
    return compress(lax.psum(local_gram, "space"))


def apply_coefficients(coefficients, stacked, weighted):
    basis = jnp.dot(coefficients.T, stacked, preferred_element_type=jnp.float32).astype(
        jnp.bfloat16
    )
    weighted_basis = jnp.dot(coefficients.T, weighted, preferred_element_type=jnp.float32).astype(
        jnp.bfloat16
    )
    return (basis, weighted_basis)


def ordered(upper_half, own_rows, partner_rows):
    lower_part = jnp.where(upper_half, partner_rows, own_rows)
    upper_part = jnp.where(upper_half, own_rows, partner_rows)
    return jnp.concatenate([lower_part, upper_part], axis=0)


def shards(snapshots, prior_basis, mass_factor, neighbours):
    local_index = neighbours - (lax.axis_index("space") * LOCAL_BLOCKS - REACH)
    stacked = jnp.concatenate([prior_basis, snapshots], axis=0)
    weighted = weigh_rows(stacked, mass_factor, local_index)
    basis, weighted_basis = apply_coefficients(coefficients_of(weighted), stacked, weighted)
    member = lax.axis_index("tm")
    for level_bit in range(lax.axis_size("tm").bit_length() - 1):
        upper_half = member // (1 << level_bit) % 2 == 1
        partner_weighted = partner(weighted_basis, "tm", level_bit)
        weighted = ordered(upper_half, weighted_basis, partner_weighted)
        coefficients = coefficients_of(weighted)
        partner_rows = partner(basis, "tm", level_bit)
        stacked = ordered(upper_half, basis, partner_rows)
        basis, weighted_basis = apply_coefficients(coefficients, stacked, weighted)
    share_width = basis.shape[1] // lax.axis_size("tm")
    basis_share = lax.dynamic_slice_in_dim(basis, member * share_width, share_width, 1)
    weighted_share = lax.dynamic_slice_in_dim(weighted_basis, member * share_width, share_width, 1)
    return (basis_share, weighted_share)


def solution(mesh):
    return jax.shard_map(
        shards,
        mesh=mesh,
        in_specs=(P("tm", "space"), P("tm", "space"), P(None, None, "space"), P("space", None)),
        out_specs=(P(None, ("space", "tm")), P(None, ("space", "tm"))),
        check_vma=False,
    )
```

profile of v0, /device:TPU:1, one launch (start us, length us, event | category | flops | bytes accessed | tf_op | source)
XLA Modules:
  0.0 817.4 jit_solution(14722766213442780236)
XLA Ops:
  19.5 20.9 %reshape.97 = bf16[7,64,128,64]{3,2,1,0:T(8,128)(2,1)} reshape(bf16[7,64,8192]{2,1,0:T(8,128)(2,1)} %param.9) | data formatting | bytes 14680064 | tf_op jit(solution)/shard_map/reshape | solution.py:42
  40.5 6.7 pad_maximum_fusion
  47.1 22.8 %gather_fusion = bf16[896,128,64]{1,2,0:T(8,128)(2,1)} fusion(bf16[128,144,64]{0,2,1:T(8,128)(2,1)S(1)} %bitcast.178, s32[1024]{0:T(1024)S(1)} %pad_clamp_fusion), kind=kCustom, calls=%fused_computation | custom fusion | bytes 29363712 | tf_op jit(solution)/shard_map/jit(_take)/gather | solution.py:41
  69.9 29.0 %bitcast_convert_fusion = bf16[128,128,64]{1,2,0:T(8,128)(2,1)S(1)} fusion(bf16[128,7,128,64]{2,3,1,0:T(8,128)(2,1)} %bitcast.179, pred[128,7]{1,0:T(8,128)(4,1)S(1)} %copy.29, bf16[7,64,128,64]{3,2,1,0:T(8,128)(2,1)} %reshape.97), kind=kOutput, calls=%fused_computation.20 | convolution fusion | flops 947912704 | bytes 24118144 | tf_op jit(solution)/shard_map/cbkq,kqbr->cbr/dot_general | solution.py:43
  100.4 174.6 %all-reduce.4.cloned.1.call-done = f32[128,128]{1,0:T(8,128)} async-done(((f32[128,128]{1,0:T(8,128)}), f32[128,128]{1,0:T(8,128)}) %all-reduce.4.cloned.1.call-update) | async-done | bytes 65552 | tf_op jit(solution)/shard_map/psum | solution.py:69
  278.5 5.8 cholesky.149
  285.7 4.9 custom-call.31
  294.4 5.8 cholesky.160
  308.6 5.8 cholesky.171
  315.8 4.9 custom-call.33
  323.5 23.1 %collective-permute-done.2 = bf16[64,8192]{1,0:T(8,128)(2,1)S(1)} collective-permute-done((bf16[64,8192]{1,0:T(8,128)(2,1)S(1)}, bf16[64,8192]{1,0:T(8,128)(2,1)S(1)}, u32[]{:S(2)}, u32[]{:S(2)}) %collective-permute-start.2) | collective-permute-done | bytes 1048608 | tf_op jit(solution)/shard_map/ppermute | solution.py:34
  354.2 163.1 %all-reduce.6.cloned.1.call-done = f32[128,128]{1,0:T(8,128)} async-done(((f32[128,128]{1,0:T(8,128)}), f32[128,128]{1,0:T(8,128)}) %all-reduce.6.cloned.1.call-update) | async-done | bytes 65552 | tf_op jit(solution)/shard_map/psum | solution.py:69
  520.9 5.8 cholesky.182
  528.1 4.9 custom-call.34
  536.8 5.8 cholesky.193
  551.0 5.8 cholesky.204
  558.2 4.9 custom-call.36
  570.6 20.7 %collective-permute-done.3 = bf16[64,8192]{1,0:T(8,128)(2,1)S(1)} collective-permute-done((bf16[64,8192]{1,0:T(8,128)(2,1)S(1)}, bf16[64,8192]{1,0:T(8,128)(2,1)S(1)}, u32[]{:S(2)}, u32[]{:S(2)}) %collective-permute-start.3) | collective-permute-done | bytes 1048608 | tf_op jit(solution)/shard_map/ppermute | solution.py:34
  592.9 21.1 %collective-permute-done.5 = bf16[64,8192]{1,0:T(8,128)(2,1)} collective-permute-done((bf16[64,8192]{1,0:T(8,128)(2,1)S(1)}, bf16[64,8192]{1,0:T(8,128)(2,1)}, u32[]{:S(2)}, u32[]{:S(2)}) %collective-permute-start.5) | collective-permute-done | bytes 1048608 | tf_op jit(solution)/shard_map/ppermute | solution.py:34
  616.6 145.8 %all-reduce.8.cloned.1.call-done = f32[128,128]{1,0:T(8,128)} async-done(((f32[128,128]{1,0:T(8,128)}), f32[128,128]{1,0:T(8,128)}) %all-reduce.8.cloned.1.call-update) | async-done | bytes 65552 | tf_op jit(solution)/shard_map/psum | solution.py:69
  766.0 5.8 cholesky.215
  781.8 5.8 cholesky.226
  789.0 4.9 custom-call.38
  796.0 5.8 cholesky.237
  (189 shorter events, 97.7 us)
Async XLA Ops:
  7.2 2.2 copy-start.5
  7.2 267.8 %all-reduce.4.cloned.1.call-start = ((), (), s32[]{:S(2)}) async-start(), calls=%async_computation | async-start | bytes 131072 | tf_op jit(solution)/shard_map/psum | solution.py:69
  9.3 3.2 copy-start
  11.4 7.7 copy-start.11
  12.5 27.9 %collective-permute-start = (bf16[128,512]{0,1:T(8,128)(2,1)S(1)}, bf16[128,512]{0,1:T(8,128)(2,1)S(1)}, u32[]{:S(2)}, u32[]{:S(2)}) collective-permute-start(bf16[128,512]{0,1:T(8,128)(2,1)S(1)} %get-tuple-element.6), channel_id=1, source_target_pairs={{0,4},{4,8},{8,12},{12,16},{16,20},{20,24},{24,28},{28,32},{32,36}... | collective-permute-start | bytes 393224 | tf_op jit(solution)/shard_map/ppermute | solution.py:19
  17.1 23.3 %collective-permute-start.1 = (bf16[128,512]{0,1:T(8,128)(2,1)S(1)}, bf16[128,512]{0,1:T(8,128)(2,1)S(1)}, u32[]{:S(2)}, u32[]{:S(2)}) collective-permute-start(bf16[128,512]{0,1:T(8,128)(2,1)S(1)} %get-tuple-element.7), channel_id=1, source_target_pairs={{4,0},{8,4},{12,8},{16,12},{20,16},{24,20},{28,24},{32,28},{36,32}... | collective-permute-start | bytes 393224 | tf_op jit(solution)/shard_map/ppermute | solution.py:22
  100.3 417.0 %all-reduce.6.cloned.1.call-start = ((), (), s32[]{:S(2)}) async-start(), calls=%async_computation.1 | async-start | bytes 131072 | tf_op jit(solution)/shard_map/psum | solution.py:69
  275.0 31.8 %copy-start.4 = (f32[128,128]{1,0:T(8,128)S(1)}, f32[128,128]{1,0:T(8,128)}, u32[]{:S(2)}) copy-start(f32[128,128]{1,0:T(8,128)} %all-reduce.4.cloned.1.call-done) | copy-start | bytes 196612
  322.2 24.4 %collective-permute-start.2 = (bf16[64,8192]{1,0:T(8,128)(2,1)S(1)}, bf16[64,8192]{1,0:T(8,128)(2,1)S(1)}, u32[]{:S(2)}, u32[]{:S(2)}) collective-permute-start(bf16[64,8192]{1,0:T(8,128)(2,1)S(1)} %convolution_convert_fusion.3), channel_id=1, source_target_pairs={{0,1},{1,0},{2,3},{3,2},{4,5},{5,4},{6,7},{7,6},{8,9},{9,8},{10,11... | collective-permute-start | bytes 3145736 | tf_op jit(solution)/shard_map/ppermute | solution.py:34
  346.8 1.0 copy-start.6
  346.8 1.4 copy-start.8
  346.8 2.8 copy-start.1
  349.5 412.9 %all-reduce.8.cloned.1.call-start = ((), (), s32[]{:S(2)}) async-start(), calls=%async_computation.2 | async-start | bytes 131072 | tf_op jit(solution)/shard_map/psum | solution.py:69
  352.5 211.2 %copy-start.7 = (bf16[64,8192]{1,0:T(8,128)(2,1)S(1)}, bf16[64,8192]{1,0:T(8,128)(2,1)}, u32[]{:S(2)}) copy-start(bf16[64,8192]{1,0:T(8,128)(2,1)} %copy-done.6) | copy-start | bytes 3145732
  352.5 215.7 %collective-permute-start.4 = (bf16[64,8192]{1,0:T(8,128)(2,1)S(1)}, bf16[64,8192]{1,0:T(8,128)(2,1)}, u32[]{:S(2)}, u32[]{:S(2)}) collective-permute-start(bf16[64,8192]{1,0:T(8,128)(2,1)S(1)} %convolution_convert_fusion.1), channel_id=1, source_target_pairs={{0,1},{1,0},{2,3},{3,2},{4,5},{5,4},{6,7},{7,6},{8,9},{9,8},{10,11... | collective-permute-start | bytes 3145736 | tf_op jit(solution)/shard_map/ppermute | solution.py:34
  517.4 31.8 %copy-start.2 = (f32[128,128]{1,0:T(8,128)S(1)}, f32[128,128]{1,0:T(8,128)}, u32[]{:S(2)}) copy-start(f32[128,128]{1,0:T(8,128)} %all-reduce.6.cloned.1.call-done) | copy-start | bytes 196612
  565.4 25.9 %collective-permute-start.3 = (bf16[64,8192]{1,0:T(8,128)(2,1)S(1)}, bf16[64,8192]{1,0:T(8,128)(2,1)S(1)}, u32[]{:S(2)}, u32[]{:S(2)}) collective-permute-start(bf16[64,8192]{1,0:T(8,128)(2,1)S(1)} %convolution_convert_fusion.2), channel_id=1, source_target_pairs={{0,2},{2,0},{1,3},{3,1},{4,6},{6,4},{5,7},{7,5},{8,10},{10,8},{9,1... | collective-permute-start | bytes 3145736 | tf_op jit(solution)/shard_map/ppermute | solution.py:34
  570.1 22.8 %copy-start.10 = (bf16[64,8192]{1,0:T(8,128)(2,1)}, bf16[64,8192]{1,0:T(8,128)(2,1)S(1)}, u32[]{:S(2)}) copy-start(bf16[64,8192]{1,0:T(8,128)(2,1)S(1)} %convolution_convert_fusion) | copy-start | bytes 3145732
  570.1 43.8 %collective-permute-start.5 = (bf16[64,8192]{1,0:T(8,128)(2,1)S(1)}, bf16[64,8192]{1,0:T(8,128)(2,1)}, u32[]{:S(2)}, u32[]{:S(2)}) collective-permute-start(bf16[64,8192]{1,0:T(8,128)(2,1)S(1)} %convolution_convert_fusion), channel_id=1, source_target_pairs={{0,2},{2,0},{1,3},{3,1},{4,6},{6,4},{5,7},{7,5},{8,10},{10,8},{9,1... | collective-permute-start | bytes 3145736 | tf_op jit(solution)/shard_map/ppermute | solution.py:34
  762.4 31.8 %copy-start.3 = (f32[128,128]{1,0:T(8,128)S(1)}, f32[128,128]{1,0:T(8,128)}, u32[]{:S(2)}) copy-start(f32[128,128]{1,0:T(8,128)} %all-reduce.8.cloned.1.call-done) | copy-start | bytes 196612
  808.1 1.2 copy-start.9
Sparse Core Ops, SparseCore 0:
  100.5 174.4 all-reduce.3
  349.6 167.6 all-reduce.5
  593.0 169.3 all-reduce.7
where the time goes:
time: 826 us; the launch traced here: 817 us
  waiting for transfers between devices  549 us (66%)
  other arithmetic  122 us (15%)
  matrix products  59.5 us (7%)
  local copies, waits for them, and re-layouts  59.3 us (7%)
  between operations  14.8 us (2%)
  starting transfers between devices  12.9 us (2%)
    psum x3, waiting for transfers between devices, coefficients_of(): return compress(lax.psum(local_gram, 'space'))  484 us
    ppermute x4, waiting for transfers between devices, partner(): return lax.ppermute(block, axis, route)  64.9 us
    another operation x27, other arithmetic, compress(): jnp.linalg.cholesky(inner_gram / (scales[:, None] * scales[None, :]))  58.7 us
    another operation x18, other arithmetic, compress(): lax.linalg.triangular_solve(factor_lower, normed, left_side=False, lower=...  49.9 us
    dot_general x1, matrix products, weigh_rows(): jnp.einsum('cbkq,kqbr->cbr', picked, factor, preferred_element_type=jnp.f...  29 us
    gather x1, local copies, waits for them, and re-layouts, weigh_rows(): picked = jnp.take(blocks, local_index, axis=1)  22.8 us
    reshape x1, local copies, waits for them, and re-layouts, weigh_rows(): factor = mass_factor.reshape(NEIGHBOURS, BLOCK_DOFS, -1, BLOCK_DOFS)  20.9 us
  transfers between devices with their start and end apart: 9, of which 6 were waited for; matrix products, arithmetic and copies ran while one was open for 10% of the time, Pallas kernels for 0%

commit v1 on v0

--- a/solution.py
+++ b/solution.py
@@ -66,7 +66,8 @@
 
 def coefficients_of(weighted):
     local_gram = jnp.dot(weighted, weighted.T, preferred_element_type=jnp.float32)
-    return compress(lax.psum(local_gram, "space"))
+    fill_leaves_now = lambda field_in, named_axis: lax.all_gather(field_in, named_axis).sum(axis=0)
+    return compress(fill_leaves_now(local_gram, "space"))
 
 
 def apply_coefficients(coefficients, stacked, weighted):

time: 826 us -> 549 us (0.66)
  waiting for transfers between devices: 549 us -> 274 us
  matrix products: 59.5 us -> 49.5 us
    psum x3 -> x0, waiting for transfers between devices: 484 us -> none  [coefficients_of(): return compress(lax.psum(local_gram, 'space'))]
    all_gather x0 -> x3, waiting for transfers between devices: none -> 184 us  [coefficients_of(): lax.all_gather(field_in, named_axis).sum(axis=0)]
    ppermute x4, waiting for transfers between devices: 64.9 us -> 90.7 us  [partner(): return lax.ppermute(block, axis, route)]
  transfers between devices with their start and end apart: 9 -> 9, of which waited for: 6 -> 7; matrix products, arithmetic and copies ran while one was open for 10% -> 5% of each run, Pallas kernels for 0% -> 0%
where the time goes in v1:
time: 549 us; the launch traced here: 541 us
  waiting for transfers between devices  274 us (50%)
  other arithmetic  128 us (23%)
  local copies, waits for them, and re-layouts  58.8 us (11%)
  matrix products  49.5 us (9%)
  starting transfers between devices  15.3 us (3%)
  between operations  14.7 us (3%)
    all_gather x3, waiting for transfers between devices, coefficients_of(): lax.all_gather(field_in, named_axis).sum(axis=0)  184 us
    ppermute x4, waiting for transfers between devices, partner(): return lax.ppermute(block, axis, route)  90.7 us
    another operation x27, other arithmetic, compress(): jnp.linalg.cholesky(inner_gram / (scales[:, None] * scales[None, :]))  58.7 us
    another operation x18, other arithmetic, compress(): lax.linalg.triangular_solve(factor_lower, normed, left_side=False, lower=...  49.9 us
    dot_general x1, matrix products, weigh_rows(): jnp.einsum('cbkq,kqbr->cbr', picked, factor, preferred_element_type=jnp.f...  29 us
    gather x1, local copies, waits for them, and re-layouts, weigh_rows(): picked = jnp.take(blocks, local_index, axis=1)  22.8 us
    reshape x1, local copies, waits for them, and re-layouts, weigh_rows(): factor = mass_factor.reshape(NEIGHBOURS, BLOCK_DOFS, -1, BLOCK_DOFS)  20.9 us
  transfers between devices with their start and end apart: 9, of which 7 were waited for; matrix products, arithmetic and copies ran while one was open for 5% of the time, Pallas kernels for 0%

profile of v1, /device:TPU:1, one launch (start us, length us, event | category | flops | bytes accessed | tf_op | source)
XLA Modules:
  0.0 541.3 jit_solution(17736405803509556532)
XLA Ops:
  19.5 20.9 %reshape.97 = bf16[7,64,128,64]{3,2,1,0:T(8,128)(2,1)} reshape(bf16[7,64,8192]{2,1,0:T(8,128)(2,1)} %param.9) | data formatting | bytes 14680064 | tf_op jit(solution)/shard_map/reshape | solution.py:42
  40.5 6.7 %pad_maximum_fusion = bf16[128,9216]{0,1:T(8,128)(2,1)S(1)} fusion(bf16[128,512]{0,1:T(8,128)(2,1)S(1)} %collective-permute-done.1, bf16[64,8192]{0,1:T(8,128)(2,1)} %copy.31, bf16[64,8192]{0,1:T(8,128)(2,1)} %copy-done, bf16[128,512]{0,1:T(8,128)(2,1)S(1)} %collective-permute-done), kind=kLoop, calls=%fused_computation.21 | loop fusion | flops 9437184 | bytes 4718592 | tf_op jit(solution)/shard_map/concatenate | solution.py:23
  47.1 22.8 %gather_fusion = bf16[896,128,64]{1,2,0:T(8,128)(2,1)} fusion(bf16[128,144,64]{0,2,1:T(8,128)(2,1)S(1)} %bitcast.181, s32[1024]{0:T(1024)S(1)} %pad_clamp_fusion), kind=kCustom, calls=%fused_computation | custom fusion | bytes 29363712 | tf_op jit(solution)/shard_map/jit(_take)/gather | solution.py:41
  69.9 29.0 %bitcast_convert_fusion = bf16[128,128,64]{1,2,0:T(8,128)(2,1)S(1)} fusion(bf16[128,7,128,64]{2,3,1,0:T(8,128)(2,1)} %bitcast.182, pred[128,7]{1,0:T(8,128)(4,1)S(1)} %copy.29, bf16[7,64,128,64]{3,2,1,0:T(8,128)(2,1)} %reshape.97), kind=kOutput, calls=%fused_computation.20 | convolution fusion | flops 947912704 | bytes 24118144 | tf_op jit(solution)/shard_map/cbkq,kqbr->cbr/dot_general | solution.py:43
  100.4 83.2 %all-gather.7.cloned.1.call-done = f32[8192,128]{1,0:T(8,128)} async-done(((f32[128,128]{1,0:T(8,128)}), f32[8192,128]{1,0:T(8,128)}) %all-gather.7.cloned.1.call-update) | async-done | bytes 4194320 | tf_op jit(solution)/shard_map/all_gather | solution.py:69
  187.9 5.8 %cholesky.149 = f32[64,64]{1,0:T(8,128)S(1)} custom-call(f32[64,64]{1,0:T(8,128)S(1)} %fusion.60), custom_call_target="Cholesky" | custom-call | tf_op jit(solution)/shard_map/jit(cholesky)/cholesky | solution.py:57
  202.0 5.8 %cholesky.160 = f32[64,64]{1,0:T(8,128)S(1)} custom-call(f32[64,64]{1,0:T(8,128)S(1)} %fusion.58), custom_call_target="Cholesky" | custom-call | tf_op jit(solution)/shard_map/jit(cholesky)/cholesky | solution.py:57
  209.2 4.9 custom-call.32
  216.2 5.8 %cholesky.171 = f32[64,64]{1,0:T(8,128)S(1)} custom-call(f32[64,64]{1,0:T(8,128)S(1)} %fusion.56), custom_call_target="Cholesky" | custom-call | tf_op jit(solution)/shard_map/jit(cholesky)/cholesky | solution.py:57
  231.1 23.4 %collective-permute-done.2 = bf16[64,8192]{1,0:T(8,128)(2,1)} collective-permute-done((bf16[64,8192]{1,0:T(8,128)(2,1)S(1)}, bf16[64,8192]{1,0:T(8,128)(2,1)}, u32[]{:S(2)}, u32[]{:S(2)}) %collective-permute-start.2) | collective-permute-done | bytes 1048608 | tf_op jit(solution)/shard_map/ppermute | solution.py:34
  257.7 76.7 %all-gather.9.cloned.1.call-done = f32[8192,128]{1,0:T(8,128)} async-done(((f32[128,128]{1,0:T(8,128)}), f32[8192,128]{1,0:T(8,128)}) %all-gather.9.cloned.1.call-update) | async-done | bytes 4194320 | tf_op jit(solution)/shard_map/all_gather | solution.py:69
  338.6 5.8 %cholesky.182 = f32[64,64]{1,0:T(8,128)S(1)} custom-call(f32[64,64]{1,0:T(8,128)S(1)} %fusion.54), custom_call_target="Cholesky" | custom-call | tf_op jit(solution)/shard_map/jit(cholesky)/cholesky | solution.py:57
  352.8 5.8 %cholesky.193 = f32[64,64]{1,0:T(8,128)S(1)} custom-call(f32[64,64]{1,0:T(8,128)S(1)} %fusion.52), custom_call_target="Cholesky" | custom-call | tf_op jit(solution)/shard_map/jit(cholesky)/cholesky | solution.py:57
  360.0 4.9 custom-call.35
  367.0 5.8 %cholesky.204 = f32[64,64]{1,0:T(8,128)S(1)} custom-call(f32[64,64]{1,0:T(8,128)S(1)} %fusion.50), custom_call_target="Cholesky" | custom-call | tf_op jit(solution)/shard_map/jit(cholesky)/cholesky | solution.py:57
  383.0 23.2 %collective-permute-done.3 = bf16[64,8192]{1,0:T(8,128)(2,1)S(1)} collective-permute-done((bf16[64,8192]{1,0:T(8,128)(2,1)S(1)}, bf16[64,8192]{1,0:T(8,128)(2,1)S(1)}, u32[]{:S(2)}, u32[]{:S(2)}) %collective-permute-start.3) | collective-permute-done | bytes 1048608 | tf_op jit(solution)/shard_map/ppermute | solution.py:34
  413.1 22.5 %collective-permute-done.4 = bf16[64,8192]{1,0:T(8,128)(2,1)S(1)} collective-permute-done((bf16[64,8192]{1,0:T(8,128)(2,1)S(1)}, bf16[64,8192]{1,0:T(8,128)(2,1)S(1)}, u32[]{:S(2)}, u32[]{:S(2)}) %collective-permute-start.4) | collective-permute-done | bytes 1048608 | tf_op jit(solution)/shard_map/ppermute | solution.py:34
  439.1 21.6 %collective-permute-done.5 = bf16[64,8192]{1,0:T(8,128)(2,1)S(1)} collective-permute-done((bf16[64,8192]{1,0:T(8,128)(2,1)S(1)}, bf16[64,8192]{1,0:T(8,128)(2,1)S(1)}, u32[]{:S(2)}, u32[]{:S(2)}) %collective-permute-start.5) | collective-permute-done | bytes 1048608 | tf_op jit(solution)/shard_map/ppermute | solution.py:34
  462.2 23.7 %all-gather.11.cloned.1.call-done = f32[8192,128]{1,0:T(8,128)} async-done(((f32[128,128]{1,0:T(8,128)}), f32[8192,128]{1,0:T(8,128)}) %all-gather.11.cloned.1.call-update) | async-done | bytes 4194320 | tf_op jit(solution)/shard_map/all_gather | solution.py:69
  490.1 5.8 %cholesky.215 = f32[64,64]{1,0:T(8,128)S(1)} custom-call(f32[64,64]{1,0:T(8,128)S(1)} %fusion.48), custom_call_target="Cholesky" | custom-call | tf_op jit(solution)/shard_map/jit(cholesky)/cholesky | solution.py:57
  497.3 4.9 custom-call.37
  504.3 5.8 %cholesky.226 = f32[64,64]{1,0:T(8,128)S(1)} custom-call(f32[64,64]{1,0:T(8,128)S(1)} %fusion.46), custom_call_target="Cholesky" | custom-call | tf_op jit(solution)/shard_map/jit(cholesky)/cholesky | solution.py:57
  518.5 5.8 %cholesky.237 = f32[64,64]{1,0:T(8,128)S(1)} custom-call(f32[64,64]{1,0:T(8,128)S(1)} %fusion.44), custom_call_target="Cholesky" | custom-call | tf_op jit(solution)/shard_map/jit(cholesky)/cholesky | solution.py:57
  525.7 4.9 custom-call.39
  (180 shorter events, 100.6 us)
Async XLA Ops:
  7.2 2.2 copy-start.2
  7.2 176.5 %all-gather.7.cloned.1.call-start = ((), (), s32[]{:S(2)}) async-start(), calls=%async_computation | async-start | bytes 4259840 | tf_op jit(solution)/shard_map/all_gather | solution.py:69
  9.3 3.2 copy-start
  11.4 7.7 %copy-start.5 = (s32[128,7]{0,1:T(8,128)S(1)}, s32[128,7]{0,1:T(8,128)}, u32[]{:S(2)}) copy-start(s32[128,7]{0,1:T(8,128)} %param.10) | copy-start | bytes 10756
  12.5 27.9 %collective-permute-start = (bf16[128,512]{0,1:T(8,128)(2,1)S(1)}, bf16[128,512]{0,1:T(8,128)(2,1)S(1)}, u32[]{:S(2)}, u32[]{:S(2)}) collective-permute-start(bf16[128,512]{0,1:T(8,128)(2,1)S(1)} %get-tuple-element.6), channel_id=1, source_target_pairs={{0,4},{4,8},{8,12},{12,16},{16,20},{20,24},{24,28},{28,32},{32,36}... | collective-permute-start | bytes 393224 | tf_op jit(solution)/shard_map/ppermute | solution.py:19
  17.1 23.3 %collective-permute-start.1 = (bf16[128,512]{0,1:T(8,128)(2,1)S(1)}, bf16[128,512]{0,1:T(8,128)(2,1)S(1)}, u32[]{:S(2)}, u32[]{:S(2)}) collective-permute-start(bf16[128,512]{0,1:T(8,128)(2,1)S(1)} %get-tuple-element.7), channel_id=1, source_target_pairs={{4,0},{8,4},{12,8},{16,12},{20,16},{24,20},{28,24},{32,28},{36,32}... | collective-permute-start | bytes 393224 | tf_op jit(solution)/shard_map/ppermute | solution.py:22
  100.3 234.1 %all-gather.9.cloned.1.call-start = ((), (), s32[]{:S(2)}) async-start(), calls=%async_computation.1 | async-start | bytes 4259840 | tf_op jit(solution)/shard_map/all_gather | solution.py:69
  229.9 24.6 %collective-permute-start.2 = (bf16[64,8192]{1,0:T(8,128)(2,1)S(1)}, bf16[64,8192]{1,0:T(8,128)(2,1)}, u32[]{:S(2)}, u32[]{:S(2)}) collective-permute-start(bf16[64,8192]{1,0:T(8,128)(2,1)S(1)} %convolution_convert_fusion.3), channel_id=1, source_target_pairs={{0,1},{1,0},{2,3},{3,2},{4,5},{5,4},{6,7},{7,6},{8,9},{9,8},{10,11... | collective-permute-start | bytes 3145736 | tf_op jit(solution)/shard_map/ppermute | solution.py:34
  257.2 228.7 %all-gather.11.cloned.1.call-start = ((), (), s32[]{:S(2)}) async-start(), calls=%async_computation.2 | async-start | bytes 4259840 | tf_op jit(solution)/shard_map/all_gather | solution.py:69
  380.2 26.0 %collective-permute-start.3 = (bf16[64,8192]{1,0:T(8,128)(2,1)S(1)}, bf16[64,8192]{1,0:T(8,128)(2,1)S(1)}, u32[]{:S(2)}, u32[]{:S(2)}) collective-permute-start(bf16[64,8192]{1,0:T(8,128)(2,1)S(1)} %convolution_convert_fusion.2), channel_id=1, source_target_pairs={{0,2},{2,0},{1,3},{3,1},{4,6},{6,4},{5,7},{7,5},{8,10},{10,8},{9,1... | collective-permute-start | bytes 3145736 | tf_op jit(solution)/shard_map/ppermute | solution.py:34
  406.4 1.0 copy-start.3
  406.4 2.3 copy-start.1
  411.7 23.9 %collective-permute-start.4 = (bf16[64,8192]{1,0:T(8,128)(2,1)S(1)}, bf16[64,8192]{1,0:T(8,128)(2,1)S(1)}, u32[]{:S(2)}, u32[]{:S(2)}) collective-permute-start(bf16[64,8192]{1,0:T(8,128)(2,1)S(1)} %convolution_convert_fusion.1), channel_id=1, source_target_pairs={{0,1},{1,0},{2,3},{3,2},{4,5},{5,4},{6,7},{7,6},{8,9},{9,8},{10,11... | collective-permute-start | bytes 3145736 | tf_op jit(solution)/shard_map/ppermute | solution.py:34
  436.3 24.4 %collective-permute-start.5 = (bf16[64,8192]{1,0:T(8,128)(2,1)S(1)}, bf16[64,8192]{1,0:T(8,128)(2,1)S(1)}, u32[]{:S(2)}, u32[]{:S(2)}) collective-permute-start(bf16[64,8192]{1,0:T(8,128)(2,1)S(1)} %convolution_convert_fusion), channel_id=1, source_target_pairs={{0,2},{2,0},{1,3},{3,1},{4,6},{6,4},{5,7},{7,5},{8,10},{10,8},{9,1... | collective-permute-start | bytes 3145736 | tf_op jit(solution)/shard_map/ppermute | solution.py:34
  488.3 42.9 %copy-start.4 = (bf16[64,8192]{1,0:T(8,128)(2,1)S(1)}, bf16[64,8192]{1,0:T(8,128)(2,1)}, u32[]{:S(2)}) copy-start(bf16[64,8192]{1,0:T(8,128)(2,1)} %copy-done.3) | copy-start | bytes 3145732
Sparse Core Ops, SparseCore 0:
  100.5 83.1 all-gather.6
  257.3 77.0 all-gather.8
  408.8 77.0 all-gather.10
